TPU v7x, 32 devices: a whole 2x2x4 slice. The times are simulated.
32 devices in a mesh: blk: 16 (over z, y, core), rel: 2 (over x).
Axes of the slice: x: 2, y: 2, z: 4, core: 2. Of those that a mesh axis runs over, the one named last changes fastest.
Arguments:
- user_table: float32 [16384, 512], P(('blk', 'rel')), may hold values from -1.5 to 1.5
- user_accum: float32 [16384], P(('blk', 'rel')), may hold values from 1 to 100
- item_table: float32 [32768, 512], P(('blk', 'rel')), may hold values from -1.5 to 1.5
- item_accum: float32 [32768], P(('blk', 'rel')), may hold values from 1 to 100
- relation: bfloat16 [512, 512], replicated, may hold values from -0.25 to 0.25
- relation_accum: float32 [512], replicated, may hold values from 0.5 to 8
- targets: bfloat16 [2, 16384, 2048], P(None, 'blk', 'rel'), may hold values from 0 to 1
Outputs:
- user_table_next: float32 [16384, 512], P(('blk', 'rel'))
- user_accum_next: float32 [16384], P(('blk', 'rel'))
- item_table_next: float32 [32768, 512], P(('blk', 'rel'))
- item_accum_next: float32 [32768], P(('blk', 'rel'))
- relation_step: float32 [512, 512], replicated
- relation_accum_next: float32 [512], replicated
All inputs are finite; a program needn't handle non-finite values.
Results may differ from a plain program's by a relative error of at most 0.0037.
The roundings to bfloat16 on the way count: a program that leaves them out, or rounds other values in their place, can miss the bound.
Values may be sent and summed in bfloat16 or wider, within the bound.
No kernel may reach another device: no remote copies, remote signals or barrier semaphores. Data moves between devices by JAX's collectives and lax.ppermute only.
A program may use at most 64 MiB of HBM per device.

v0:
```python
import jax
import jax.numpy as jnp
from jax import lax
from jax.sharding import PartitionSpec as P

learn_rate = 0.1
epsilon = 1e-06


def from_behind(shard, axis, by):
    peers = lax.axis_size(axis)
    return lax.ppermute(shard, axis, [(i, (i + by) % peers) for i in range(peers)])


def adagrad_rows(table, accum, grads):
    accum_next = accum + jnp.mean(grads * grads, axis=1)
    return (table - learn_rate * grads * lax.rsqrt(accum_next + epsilon)[:, None], accum_next)


def per_device(user_table, user_accum, item_table, item_accum, relation, relation_accum, targets):
    blocks = lax.axis_size("blk")
    rounds = targets.shape[0]
    users_now, user_sums = (user_table, user_accum)
    items_now, item_sums = (item_table, item_accum)
    relation_local = jnp.zeros((relation.shape[0], relation.shape[1]), jnp.float32)
    for turn in range(rounds):
        whole_users = lax.all_gather(users_now.astype(jnp.bfloat16), "rel", axis=0, tiled=True)
        item_bf = items_now.astype(jnp.bfloat16)
        anchor = jnp.dot(whole_users, relation, preferred_element_type=jnp.float32).astype(
            jnp.bfloat16
        )
        scores = lax.dot_general(
            anchor, item_bf, (((1,), (1,)), ((), ())), preferred_element_type=jnp.float32
        )
        errors = (jax.nn.sigmoid(scores) - targets[turn].astype(jnp.float32)).astype(jnp.bfloat16)
        mapped = lax.dot_general(
            item_bf, relation, (((1,), (1,)), ((), ())), preferred_element_type=jnp.float32
        ).astype(jnp.bfloat16)
        user_grad = lax.psum_scatter(
            jnp.dot(errors, mapped, preferred_element_type=jnp.float32),
            "rel",
            scatter_dimension=0,
            tiled=True,
        )
        item_grad = lax.dot_general(
            errors, anchor, (((0,), (0,)), ((), ())), preferred_element_type=jnp.float32
        )
        crossed = lax.dot_general(
            whole_users, errors, (((0,), (0,)), ((), ())), preferred_element_type=jnp.float32
        ).astype(jnp.bfloat16)
        term = jnp.dot(crossed, item_bf, preferred_element_type=jnp.float32)
        relation_local = relation_local + term
        users_now, user_sums = adagrad_rows(users_now, user_sums, user_grad)
        items_now, item_sums = adagrad_rows(items_now, item_sums, item_grad)
        items_now, item_sums = from_behind((items_now, item_sums), "blk", 1)
    total = lax.psum(relation_local, ("blk", "rel"))
    mean_grad = total / (blocks * rounds)
    accum_next = relation_accum + jnp.mean(mean_grad * mean_grad, axis=1)
    relation_step = mean_grad * lax.rsqrt(accum_next + epsilon)[:, None]
    return (users_now, user_sums, items_now, item_sums, relation_step, accum_next)


def solution(mesh):
    return jax.shard_map(
        per_device,
        mesh=mesh,
        in_specs=(
            P(("blk", "rel"), None),
            P(("blk", "rel")),
            P(("blk", "rel"), None),
            P(("blk", "rel")),
            P(),
            P(),
            P(None, "blk", "rel"),
        ),
        out_specs=(
            P(("blk", "rel"), None),
            P(("blk", "rel")),
            P(("blk", "rel"), None),
            P(("blk", "rel")),
            P(),
            P(),
        ),
        check_vma=False,
    )
```

profile of v0, /device:TPU:0, one launch (start us, length us, event | category | flops | bytes accessed | tf_op | source)
XLA Modules:
  0.0 306.9 jit_solution(6745645054614576776)
XLA Ops:
  7.2 2.1 convert_element_type.49
  9.4 24.7 %all-gather.3.cloned.1.call-done = bf16[1024,512]{1,0:T(8,128)(2,1)} async-done(((bf16[512,512]{1,0:T(8,128)(2,1)}), bf16[1024,512]{1,0:T(8,128)(2,1)}) %all-gather.3.cloned.1.call-update) | async-done | bytes 1048592 | tf_op jit(solution)/shard_map/all_gather | solution.py:27
  34.1 1.9 convolution_convert_fusion.5
  36.1 5.2 %fusion.1 = bf16[1024,1024]{1,0:T(8,128)(2,1)} fusion(bf16[1024,512]{1,0:T(8,128)(2,1)S(1)} %convolution_convert_fusion.5, bf16[2,1024,1024]{2,1,0:T(8,128)(2,1)} %param.13, f32[1024,512]{1,0:T(8,128)} %param.9), kind=kOutput, calls=%fused_computation.3 | convolution fusion | flops 1080557568 | bytes 7340032 | tf_op jit(solution)/shard_map/dot_general | solution.py:32
  41.3 5.4 %fusion.2 = f32[1024,512]{1,0:T(8,128)} fusion(bf16[1024,1024]{1,0:T(8,128)(2,1)} %fusion.1, bf16[512,512]{1,0:T(8,128)(2,1)S(1)} %copy-done, f32[1024,512]{1,0:T(8,128)} %param.9), kind=kOutput, calls=%fused_computation.20 | convolution fusion | flops 1611661312 | bytes 6815744 | tf_op jit(solution)/shard_map/dot_general | solution.py:40
  46.8 2.9 copy.13
  49.7 3.0 multiply_reduce_fusion.1
  52.8 1.8 multiply_subtract_fusion.1
  54.6 24.2 %reduce-scatter.3.cloned.1.call-done = f32[512,512]{1,0:T(8,128)} async-done(((f32[1024,512]{1,0:T(8,128)}), f32[512,512]{1,0:T(8,128)}) %reduce-scatter.3.cloned.1.call-update) | async-done | bytes 1048592 | tf_op jit(solution)/shard_map/reduce_scatter | solution.py:39
  78.8 1.4 multiply_reduce_fusion.4
  80.2 2.2 fusion.5
  82.4 5.3 %fusion.4 = f32[512,512]{1,0:T(8,128)} fusion(bf16[1024,1024]{1,0:T(8,128)(2,1)} %fusion.1, bf16[1024,512]{1,0:T(8,128)(2,1)} %all-gather.3.cloned.1.call-done, f32[1024,512]{1,0:T(8,128)} %param.9), kind=kOutput, calls=%fused_computation.22 | convolution fusion | flops 1611661312 | bytes 6291456 | tf_op jit(solution)/shard_map/dot_general | solution.py:51
  87.8 16.0 %all-gather.5.cloned.1.call-done = bf16[1024,512]{1,0:T(8,128)(2,1)} async-done(((bf16[512,512]{1,0:T(8,128)(2,1)}), bf16[1024,512]{1,0:T(8,128)(2,1)}) %all-gather.5.cloned.1.call-update) | async-done | bytes 1048592 | tf_op jit(solution)/shard_map/all_gather | solution.py:27
  103.8 1.9 convolution_convert_fusion.3
  105.8 0.9 copy-done.7
  106.7 5.2 %fusion = bf16[1024,1024]{1,0:T(8,128)(2,1)} fusion(bf16[1024,512]{1,0:T(8,128)(2,1)S(1)} %convolution_convert_fusion.3, bf16[2,1024,1024]{2,1,0:T(8,128)(2,1)} %param.13, f32[1024,512]{0,1:T(8,128)} %collective-permute-done), kind=kOutput, calls=%fused_computation.1 | convolution fusion | flops 1080557568 | bytes 7340032 | tf_op jit(solution)/shard_map/dot_general | solution.py:32
  111.9 5.6 %convolution_add_fusion = f32[512,512]{1,0:T(8,128)} fusion(f32[512,512]{1,0:T(8,128)} %fusion.4, bf16[1024,512]{1,0:T(8,128)(2,1)} %all-gather.5.cloned.1.call-done, bf16[1024,1024]{1,0:T(8,128)(2,1)} %fusion, f32[1024,512]{0,1:T(8,128)} %collective-permute-done), kind=kOutput, calls=%fused_computation.14 | convolution fusion | flops 1611923456 | bytes 7340032 | tf_op jit(solution)/shard_map/dot_general | solution.py:51
  117.8 5.4 %fusion.3 = f32[1024,512]{1,0:T(8,128)} fusion(bf16[1024,1024]{1,0:T(8,128)(2,1)} %fusion, bf16[512,512]{1,0:T(8,128)(2,1)S(1)} %copy-done, f32[1024,512]{0,1:T(8,128)} %collective-permute-done), kind=kOutput, calls=%fused_computation.21 | convolution fusion | flops 1611661312 | bytes 6815744 | tf_op jit(solution)/shard_map/dot_general | solution.py:40
  123.2 3.2 %multiply_reduce_fusion = (f32[1024]{0:T(1024)S(1)}, f32[1024,512]{0,1:T(8,128)S(1)}) fusion(bf16[1024,1024]{1,0:T(8,128)(2,1)} %fusion, bf16[1024,512]{1,0:T(8,128)(2,1)} %copy-done.7), kind=kOutput, calls=%fused_computation.5 | convolution fusion | flops 1074789376 | bytes 5246976 | tf_op jit(solution)/shard_map/dot_general | solution.py:45
  126.4 2.6 collective-permute-done.1
  129.0 3.4 %multiply_subtract_fusion = f32[1024,512]{0,1:T(8,128)} fusion(f32[1024,512]{0,1:T(8,128)} %collective-permute-done, f32[1024,512]{0,1:T(8,128)S(1)} %get-tuple-element.23, f32[1024]{0:T(1024)S(1)} %get-tuple-element.14), kind=kLoop, calls=%fused_computation.4 | loop fusion | flops 1048576 | bytes 6295552 | tf_op jit(solution)/shard_map/sub | solution.py:17
  132.4 30.8 %collective-permute-done.3 = f32[1024]{0:T(1024)S(1)} collective-permute-done((f32[1024]{0:T(1024)S(1)}, f32[1024]{0:T(1024)S(1)}, u32[]{:S(2)}, u32[]{:S(2)}) %collective-permute-start.3) | collective-permute-done | bytes 4128 | tf_op jit(solution)/shard_map/ppermute | solution.py:12
  163.2 99.2 %all-reduce.2.cloned.1.call-done = f32[512,512]{1,0:T(8,128)} async-done(((f32[512,512]{1,0:T(8,128)}), f32[512,512]{1,0:T(8,128)}) %all-reduce.2.cloned.1.call-update) | async-done | bytes 1048592 | tf_op jit(solution)/shard_map/psum | solution.py:56
  262.4 1.4 multiply_reduce_fusion.2
  263.8 0.6 rsqrt_multiply_fusion.2
  264.4 2.3 broadcast_multiply_fusion
  266.8 3.0 copy.14
  269.7 25.7 %reduce-scatter.5.cloned.1.call-done = f32[512,512]{1,0:T(8,128)} async-done(((f32[1024,512]{1,0:T(8,128)}), f32[512,512]{1,0:T(8,128)}) %reduce-scatter.5.cloned.1.call-update) | async-done | bytes 1048592 | tf_op jit(solution)/shard_map/reduce_scatter | solution.py:39
  295.4 1.4 multiply_reduce_fusion.3
  296.8 0.6 rsqrt_multiply_fusion.3
  297.4 2.4 multiply_subtract_fusion.2
  299.8 0.6 copy.17
  (34 shorter events, 0.6 us)
Async XLA Ops:
  7.2 27.0 %copy-start = (bf16[512,512]{1,0:T(8,128)(2,1)S(1)}, bf16[512,512]{1,0:T(8,128)(2,1)}, u32[]{:S(2)}) copy-start(bf16[512,512]{1,0:T(8,128)(2,1)} %param.11) | copy-start | bytes 1572868
  7.2 27.0 %all-gather.3.cloned.1.call-start = ((), (), s32[]{:S(2)}) async-start(), calls=%async_computation.2 | async-start | bytes 1572864 | tf_op jit(solution)/shard_map/all_gather | solution.py:27
  9.4 69.4 %reduce-scatter.3.cloned.1.call-start = ((), (), s32[]{:S(2)}) async-start(), calls=%async_computation.3 | async-start | bytes 3145728 | tf_op jit(solution)/shard_map/reduce_scatter | solution.py:39
  46.7 57.1 %all-gather.5.cloned.1.call-start = ((), (), s32[]{:S(2)}) async-start(), calls=%async_computation.4 | async-start | bytes 1572864 | tf_op jit(solution)/shard_map/all_gather | solution.py:27
  49.7 3.0 copy-start.5
  49.7 3.1 %copy-start.3 = (f32[1024,512]{0,1:T(8,128)S(1)}, f32[1024,512]{0,1:T(8,128)}, u32[]{:S(2)}) copy-start(f32[1024,512]{0,1:T(8,128)} %copy.13) | copy-start | bytes 6291460
  52.8 27.4 %copy-start.4 = (f32[512]{0:T(512)S(1)}, f32[512]{0:T(512)}, u32[]{:S(2)}) copy-start(f32[512]{0:T(512)} %param.8) | copy-start | bytes 6148
  52.8 27.4 %copy-start.1 = (f32[512,512]{1,0:T(8,128)S(1)}, f32[512,512]{1,0:T(8,128)}, u32[]{:S(2)}) copy-start(f32[512,512]{1,0:T(8,128)} %param.7) | copy-start | bytes 3145732
  54.6 51.2 %collective-permute-start = (f32[1024,512]{0,1:T(8,128)}, f32[1024,512]{0,1:T(8,128)}, u32[]{:S(2)}, u32[]{:S(2)}) collective-permute-start(f32[1024,512]{0,1:T(8,128)} %multiply_subtract_fusion.1), channel_id=1, source_target_pairs={{0,2},{2,4},{4,6},{6,8},{8,10},{10,12},{12,14},{14,16},{16,18},{18... | collective-permute-start | bytes 6291464 | tf_op jit(solution)/shard_map/ppermute | solution.py:12
  82.4 180.0 %all-reduce.2.cloned.1.call-start = ((), (), s32[]{:S(2)}) async-start(), calls=%async_computation.6 | async-start | bytes 2097152 | tf_op jit(solution)/shard_map/psum | solution.py:56
  105.7 1.0 copy-start.7
  117.5 177.9 %reduce-scatter.5.cloned.1.call-start = ((), (), s32[]{:S(2)}) async-start(), calls=%async_computation.5 | async-start | bytes 3145728 | tf_op jit(solution)/shard_map/reduce_scatter | solution.py:39
  123.2 5.8 %collective-permute-start.1 = (f32[1024]{0:T(1024)S(1)}, f32[1024]{0:T(1024)S(1)}, u32[]{:S(2)}, u32[]{:S(2)}) collective-permute-start(f32[1024]{0:T(1024)S(1)} %get-tuple-element.19), channel_id=1, source_target_pairs={{0,2},{2,4},{4,6},{6,8},{8,10},{10,12},{12,14},{14,16},{16,18},{18... | collective-permute-start | bytes 12296 | tf_op jit(solution)/shard_map/ppermute | solution.py:12
  129.0 134.9 %copy-start.6 = (f32[512]{0:T(512)S(1)}, f32[512]{0:T(512)}, u32[]{:S(2)}) copy-start(f32[512]{0:T(512)} %param.12) | copy-start | bytes 6148
  132.4 134.4 %collective-permute-start.2 = (f32[1024,512]{0,1:T(8,128)}, f32[1024,512]{0,1:T(8,128)}, u32[]{:S(2)}, u32[]{:S(2)}) collective-permute-start(f32[1024,512]{0,1:T(8,128)} %multiply_subtract_fusion), channel_id=1, source_target_pairs={{0,2},{2,4},{4,6},{6,8},{8,10},{10,12},{12,14},{14,16},{16,18},{18... | collective-permute-start | bytes 6291464 | tf_op jit(solution)/shard_map/ppermute | solution.py:12
  132.4 30.8 %collective-permute-start.3 = (f32[1024]{0:T(1024)S(1)}, f32[1024]{0:T(1024)S(1)}, u32[]{:S(2)}, u32[]{:S(2)}) collective-permute-start(f32[1024]{0:T(1024)S(1)} %get-tuple-element.15), channel_id=1, source_target_pairs={{0,2},{2,4},{4,6},{6,8},{8,10},{10,12},{12,14},{14,16},{16,18},{18... | collective-permute-start | bytes 12296 | tf_op jit(solution)/shard_map/ppermute | solution.py:12
  266.8 30.6 %copy-start.2 = (f32[512,512]{1,0:T(8,128)S(1)}, f32[512,512]{1,0:T(8,128)}, u32[]{:S(2)}) copy-start(f32[512,512]{1,0:T(8,128)} %reduce-scatter.3.cloned.1.call-done) | copy-start | bytes 3145732
Sparse Core Ops, SparseCore 0:
  10.1 23.9 all-gather.2
  46.8 31.8 reduce-scatter.2
  82.5 21.2 all-gather.4
  117.6 144.7 all-reduce.1
  264.5 30.8 reduce-scatter.4
where the time goes:
time: 307 us
  waiting for transfers between devices  223 us (73%)
  matrix products  42.2 us (14%)
  other arithmetic  19.5 us (6%)
  between operations  13.9 us (5%)
  local copies, waits for them, and re-layouts  7.49 us (2%)
    psum x1, waiting for transfers between devices, per_device(): total = lax.psum(relation_local, ('blk', 'rel'))  99.2 us
    reduce_scatter x2, waiting for transfers between devices, per_device(): lax.psum_scatter(jnp.dot(errors, mapped, preferred_element_type=jnp.float...  49.9 us
    all_gather x2, waiting for transfers between devices, per_device(): lax.all_gather(users_now.astype(jnp.bfloat16), 'rel', axis=0, tiled=True)  40.7 us
    ppermute x4, waiting for transfers between devices, from_behind(): lax.ppermute(shard, axis, [(i, (i + by) % peers) for i in range(peers)])  33.4 us
    dot_general x2, matrix products, per_device(): term = jnp.dot(crossed, item_bf, preferred_element_type=jnp.float32)  10.9 us
    dot_general x2, matrix products, per_device(): jnp.dot(errors, mapped, preferred_element_type=jnp.float32)  10.7 us
    dot_general x2, matrix products, per_device(): lax.dot_general(anchor, item_bf, (((1,), (1,)), ((), ())), preferred_elem...  10.5 us
    sub x3, other arithmetic, adagrad_rows(): table - learn_rate * grads * lax.rsqrt(accum_next + epsilon)[:, None]  7.56 us
  transfers between devices with their start and end apart: 9, of which 7 were waited for; matrix products, arithmetic and copies ran while one was open for 12% of the time, Pallas kernels for 0%

commit v1 on v0

--- a/solution.py
+++ b/solution.py
@@ -1,3 +1,4 @@
+import functools
 import jax
 import jax.numpy as jnp
 from jax import lax
@@ -5,6 +6,13 @@
 
 learn_rate = 0.1
 epsilon = 1e-06
+
+
+def obtain_the_samples_all(packet, dev_axis):
+    return jnp.sum(lax.all_gather(packet, axis_name=dev_axis), axis=0)
+
+
+watch_row = functools.partial(obtain_the_samples_all, dev_axis=("blk", "rel"))
 
 
 def from_behind(shard, axis, by):
@@ -53,7 +61,7 @@
         users_now, user_sums = adagrad_rows(users_now, user_sums, user_grad)
         items_now, item_sums = adagrad_rows(items_now, item_sums, item_grad)
         items_now, item_sums = from_behind((items_now, item_sums), "blk", 1)
-    total = lax.psum(relation_local, ("blk", "rel"))
+    total = watch_row(relation_local)
     mean_grad = total / (blocks * rounds)
     accum_next = relation_accum + jnp.mean(mean_grad * mean_grad, axis=1)
     relation_step = mean_grad * lax.rsqrt(accum_next + epsilon)[:, None]

time: 307 us -> 368 us (1.20)
  waiting for transfers between devices: 223 us -> 275 us
  other arithmetic: 19.5 us -> 28.1 us
    all_gather x0 -> x1, waiting for transfers between devices: none -> 174 us  [obtain_the_samples_all(): return jnp.sum(lax.all_gather(packet, axis_name=dev_axis), axis=0)]
    psum x1 -> x0, waiting for transfers between devices: 99.2 us -> none  [per_device(): total = lax.psum(relation_local, ('blk', 'rel'))]
    reduce_scatter x2, waiting for transfers between devices: 49.9 us -> 24.2 us  [per_device(): lax.psum_scatter(jnp.dot(errors, mapped, preferred_element_type=jnp.float...]
    reduce_sum x0 -> x1, other arithmetic: none -> 12.3 us  [obtain_the_samples_all(): return jnp.sum(lax.all_gather(packet, axis_name=dev_axis), axis=0)]
    all_gather x2, waiting for transfers between devices: 40.7 us -> 46.1 us  [per_device(): lax.all_gather(users_now.astype(jnp.bfloat16), 'rel', axis=0, tiled=True)]
    unnamed x19 -> x21, local copies, waits for them, and re-layouts: 7.49 us -> 7.38 us
  transfers between devices with their start and end apart: 9 -> 9, of which waited for: 7 -> 6; matrix products, arithmetic and copies ran while one was open for 12% -> 10% of each run, Pallas kernels for 0% -> 0%
where the time goes in v1:
time: 368 us
  waiting for transfers between devices  275 us (75%)
  matrix products  42.7 us (12%)
  other arithmetic  28.1 us (8%)
  between operations  14 us (4%)
  local copies, waits for them, and re-layouts  7.38 us (2%)
    all_gather x1, waiting for transfers between devices, obtain_the_samples_all(): return jnp.sum(lax.all_gather(packet, axis_name=dev_axis), axis=0)  174 us
    all_gather x2, waiting for transfers between devices, per_device(): lax.all_gather(users_now.astype(jnp.bfloat16), 'rel', axis=0, tiled=True)  46.1 us
    ppermute x4, waiting for transfers between devices, from_behind(): lax.ppermute(shard, axis, [(i, (i + by) % peers) for i in range(peers)])  30.8 us
    reduce_scatter x2, waiting for transfers between devices, per_device(): lax.psum_scatter(jnp.dot(errors, mapped, preferred_element_type=jnp.float...  24.2 us
    reduce_sum x1, other arithmetic, obtain_the_samples_all(): return jnp.sum(lax.all_gather(packet, axis_name=dev_axis), axis=0)  12.3 us
    dot_general x2, matrix products, per_device(): term = jnp.dot(crossed, item_bf, preferred_element_type=jnp.float32)  11.4 us
    dot_general x2, matrix products, per_device(): jnp.dot(errors, mapped, preferred_element_type=jnp.float32)  10.8 us
    dot_general x2, matrix products, per_device(): lax.dot_general(anchor, item_bf, (((1,), (1,)), ((), ())), preferred_elem...  10.4 us
  transfers between devices with their start and end apart: 9, of which 6 were waited for; matrix products, arithmetic and copies ran while one was open for 10% of the time, Pallas kernels for 0%

profile of v1, /device:TPU:0, one launch (start us, length us, event | category | flops | bytes accessed | tf_op | source)
XLA Modules:
  0.0 367.8 jit_solution(9816643843975703561)
XLA Ops:
  7.2 2.1 convert_element_type.49
  9.4 24.7 %all-gather.5.cloned.1.call-done = bf16[1024,512]{1,0:T(8,128)(2,1)} async-done(((bf16[512,512]{1,0:T(8,128)(2,1)}), bf16[1024,512]{1,0:T(8,128)(2,1)}) %all-gather.5.cloned.1.call-update) | async-done | bytes 1048592 | tf_op jit(solution)/shard_map/all_gather | solution.py:35
  34.1 1.9 convolution_convert_fusion.5
  36.1 5.2 %fusion.1 = bf16[1024,1024]{1,0:T(8,128)(2,1)} fusion(bf16[1024,512]{1,0:T(8,128)(2,1)S(1)} %convolution_convert_fusion.5, bf16[2,1024,1024]{2,1,0:T(8,128)(2,1)} %param.13, f32[1024,512]{1,0:T(8,128)} %param.9), kind=kOutput, calls=%fused_computation.3 | convolution fusion | flops 1080557568 | bytes 7340032 | tf_op jit(solution)/shard_map/dot_general | solution.py:40
  41.3 5.4 %fusion.2 = f32[1024,512]{1,0:T(8,128)} fusion(bf16[1024,1024]{1,0:T(8,128)(2,1)} %fusion.1, bf16[512,512]{1,0:T(8,128)(2,1)S(1)} %copy-done, f32[1024,512]{1,0:T(8,128)} %param.9), kind=kOutput, calls=%fused_computation.20 | convolution fusion | flops 1611661312 | bytes 6815744 | tf_op jit(solution)/shard_map/dot_general | solution.py:48
  46.8 2.9 copy.13
  49.7 3.0 multiply_reduce_fusion.1
  52.8 1.8 multiply_subtract_fusion.1
  54.5 24.2 %reduce-scatter.3.cloned.1.call-done = f32[512,512]{1,0:T(8,128)} async-done(((f32[1024,512]{1,0:T(8,128)}), f32[512,512]{1,0:T(8,128)}) %reduce-scatter.3.cloned.1.call-update) | async-done | bytes 1048592 | tf_op jit(solution)/shard_map/reduce_scatter | solution.py:47
  78.8 1.4 multiply_reduce_fusion.4
  80.2 2.2 fusion.5
  82.4 21.4 %all-gather.7.cloned.1.call-done = bf16[1024,512]{1,0:T(8,128)(2,1)} async-done(((bf16[512,512]{1,0:T(8,128)(2,1)}), bf16[1024,512]{1,0:T(8,128)(2,1)}) %all-gather.7.cloned.1.call-update) | async-done | bytes 1048592 | tf_op jit(solution)/shard_map/all_gather | solution.py:35
  103.8 1.9 convolution_convert_fusion.3
  105.8 0.9 copy-done.8
  106.7 5.2 %fusion = bf16[1024,1024]{1,0:T(8,128)(2,1)} fusion(bf16[1024,512]{1,0:T(8,128)(2,1)S(1)} %convolution_convert_fusion.3, bf16[2,1024,1024]{2,1,0:T(8,128)(2,1)} %param.13, f32[1024,512]{0,1:T(8,128)} %collective-permute-done), kind=kOutput, calls=%fused_computation.1 | convolution fusion | flops 1080557568 | bytes 7340032 | tf_op jit(solution)/shard_map/dot_general | solution.py:40
  111.9 5.4 %fusion.3 = f32[1024,512]{1,0:T(8,128)} fusion(bf16[1024,1024]{1,0:T(8,128)(2,1)} %fusion, bf16[512,512]{1,0:T(8,128)(2,1)S(1)} %copy-done, f32[1024,512]{0,1:T(8,128)} %collective-permute-done), kind=kOutput, calls=%fused_computation.21 | convolution fusion | flops 1611661312 | bytes 6815744 | tf_op jit(solution)/shard_map/dot_general | solution.py:48
  117.4 0.2 all-gather.9.cloned.1.call-start
  117.6 5.4 %fusion.4 = f32[512,512]{1,0:T(8,128)} fusion(bf16[1024,1024]{1,0:T(8,128)(2,1)} %fusion.1, bf16[1024,512]{1,0:T(8,128)(2,1)} %all-gather.5.cloned.1.call-done, f32[1024,512]{1,0:T(8,128)} %param.9), kind=kOutput, calls=%fused_computation.22 | convolution fusion | flops 1611661312 | bytes 6291456 | tf_op jit(solution)/shard_map/dot_general | solution.py:59
  123.0 6.0 %convolution_add_fusion = f32[512,512]{1,0:T(8,128)} fusion(f32[512,512]{1,0:T(8,128)} %fusion.4, bf16[1024,512]{1,0:T(8,128)(2,1)} %all-gather.7.cloned.1.call-done, bf16[1024,1024]{1,0:T(8,128)(2,1)} %fusion, f32[1024,512]{0,1:T(8,128)} %collective-permute-done), kind=kOutput, calls=%fused_computation.14 | convolution fusion | flops 1611923456 | bytes 7340032 | tf_op jit(solution)/shard_map/dot_general | solution.py:59
  129.1 3.2 multiply_reduce_fusion
  132.3 2.6 collective-permute-done.1
  134.8 2.0 multiply_subtract_fusion
  137.0 28.3 %collective-permute-done.3 = f32[1024]{0:T(1024)S(1)} collective-permute-done((f32[1024]{0:T(1024)S(1)}, f32[1024]{0:T(1024)S(1)}, u32[]{:S(2)}, u32[]{:S(2)}) %collective-permute-start.3) | collective-permute-done | bytes 4128 | tf_op jit(solution)/shard_map/ppermute | solution.py:20
  165.3 2.9 copy.14
  168.2 1.4 multiply_reduce_fusion.3
  169.5 0.6 rsqrt_multiply_fusion.3
  170.1 2.4 multiply_subtract_fusion.2
  172.6 173.9 %all-gather.9.cloned.1.call-done = f32[16384,512]{1,0:T(8,128)} async-done(((f32[512,512]{1,0:T(8,128)}), f32[16384,512]{1,0:T(8,128)}) %all-gather.9.cloned.1.call-update) | async-done | bytes 33554448 | tf_op jit(solution)/shard_map/all_gather | solution.py:12
  346.5 12.3 %reduce_sum.58 = f32[512,512]{1,0:T(8,128)S(1)} reduce(f32[32,512,512]{2,1,0:T(8,128)} %bitcast.25, f32[]{:T(128)} %constant.7.clone.1), dimensions={0}, to_apply=%region_6.0 | reduce | flops 8126464 | bytes 34603012 | tf_op jit(solution)/shard_map/reduce_sum | solution.py:12
  359.0 0.6 rsqrt_multiply_fusion.2
  359.6 1.1 broadcast_multiply_fusion
  360.7 0.6 copy.16
  (37 shorter events, 0.7 us)
Async XLA Ops:
  7.2 27.0 %copy-start = (bf16[512,512]{1,0:T(8,128)(2,1)S(1)}, bf16[512,512]{1,0:T(8,128)(2,1)}, u32[]{:S(2)}) copy-start(bf16[512,512]{1,0:T(8,128)(2,1)} %param.11) | copy-start | bytes 1572868
  7.2 27.0 %all-gather.5.cloned.1.call-start = ((), (), s32[]{:S(2)}) async-start(), calls=%async_computation.2 | async-start | bytes 1572864 | tf_op jit(solution)/shard_map/all_gather | solution.py:35
  9.4 69.4 %reduce-scatter.3.cloned.1.call-start = ((), (), s32[]{:S(2)}) async-start(), calls=%async_computation.3 | async-start | bytes 3145728 | tf_op jit(solution)/shard_map/reduce_scatter | solution.py:47
  46.7 57.1 %all-gather.7.cloned.1.call-start = ((), (), s32[]{:S(2)}) async-start(), calls=%async_computation.4 | async-start | bytes 1572864 | tf_op jit(solution)/shard_map/all_gather | solution.py:35
  49.7 3.0 copy-start.6
  49.7 3.1 copy-start.4
  52.7 27.4 %copy-start.5 = (f32[512]{0:T(512)S(1)}, f32[512]{0:T(512)}, u32[]{:S(2)}) copy-start(f32[512]{0:T(512)} %param.8) | copy-start | bytes 6148
  52.8 27.4 %copy-start.2 = (f32[512,512]{1,0:T(8,128)S(1)}, f32[512,512]{1,0:T(8,128)}, u32[]{:S(2)}) copy-start(f32[512,512]{1,0:T(8,128)} %param.7) | copy-start | bytes 3145732
  54.5 51.2 %collective-permute-start = (f32[1024,512]{0,1:T(8,128)}, f32[1024,512]{0,1:T(8,128)}, u32[]{:S(2)}, u32[]{:S(2)}) collective-permute-start(f32[1024,512]{0,1:T(8,128)} %multiply_subtract_fusion.1), channel_id=1, source_target_pairs={{0,2},{2,4},{4,6},{6,8},{8,10},{10,12},{12,14},{14,16},{16,18},{18... | collective-permute-start | bytes 6291464 | tf_op jit(solution)/shard_map/ppermute | solution.py:20
  82.4 85.8 %reduce-scatter.5.cloned.1.call-start = ((), (), s32[]{:S(2)}) async-start(), calls=%async_computation.5 | async-start | bytes 3145728 | tf_op jit(solution)/shard_map/reduce_scatter | solution.py:47
  105.7 1.0 copy-start.8
  117.4 229.1 %all-gather.9.cloned.1.call-start = ((), (), s32[]{:S(2)}) async-start(), calls=%async_computation.6 | async-start | bytes 34603008 | tf_op jit(solution)/shard_map/all_gather | solution.py:12
  129.0 5.8 %collective-permute-start.1 = (f32[1024]{0:T(1024)S(1)}, f32[1024]{0:T(1024)S(1)}, u32[]{:S(2)}, u32[]{:S(2)}) collective-permute-start(f32[1024]{0:T(1024)S(1)} %get-tuple-element.19), channel_id=1, source_target_pairs={{0,2},{2,4},{4,6},{6,8},{8,10},{10,12},{12,14},{14,16},{16,18},{18... | collective-permute-start | bytes 12296 | tf_op jit(solution)/shard_map/ppermute | solution.py:20
  136.9 28.4 %collective-permute-start.2 = (f32[1024,512]{0,1:T(8,128)S(1)}, f32[1024,512]{0,1:T(8,128)}, u32[]{:S(2)}, u32[]{:S(2)}) collective-permute-start(f32[1024,512]{0,1:T(8,128)S(1)} %multiply_subtract_fusion), channel_id=1, source_target_pairs={{0,2},{2,4},{4,6},{6,8},{8,10},{10,12},{12,14},{14,16},{16,18},{18... | collective-permute-start | bytes 6291464 | tf_op jit(solution)/shard_map/ppermute | solution.py:20
  136.9 33.2 %copy-start.3 = (f32[512,512]{1,0:T(8,128)S(1)}, f32[512,512]{1,0:T(8,128)}, u32[]{:S(2)}) copy-start(f32[512,512]{1,0:T(8,128)} %reduce-scatter.3.cloned.1.call-done) | copy-start | bytes 3145732
  136.9 28.3 %collective-permute-start.3 = (f32[1024]{0:T(1024)S(1)}, f32[1024]{0:T(1024)S(1)}, u32[]{:S(2)}, u32[]{:S(2)}) collective-permute-start(f32[1024]{0:T(1024)S(1)} %get-tuple-element.15), channel_id=1, source_target_pairs={{0,2},{2,4},{4,6},{6,8},{8,10},{10,12},{12,14},{14,16},{16,18},{18... | collective-permute-start | bytes 12296 | tf_op jit(solution)/shard_map/ppermute | solution.py:20
  346.5 12.5 %copy-start.7 = (f32[512]{0:T(512)S(1)}, f32[512]{0:T(512)}, u32[]{:S(2)}) copy-start(f32[512]{0:T(512)} %param.12) | copy-start | bytes 6148
  346.5 14.8 %copy-start.1 = (bf16[512,512]{1,0:T(8,128)(2,1)S(1)}, bf16[512,512]{1,0:T(8,128)(2,1)}, u32[]{:S(2)}) copy-start(bf16[512,512]{1,0:T(8,128)(2,1)} %param.11) | copy-start | bytes 1572868
Sparse Core Ops, SparseCore 0:
  10.1 23.9 all-gather.4
  46.8 31.8 reduce-scatter.2
  82.5 21.2 all-gather.6
  117.5 31.8 reduce-scatter.4
  152.3 194.1 all-gather.8
